TPU v7x, 256 devices: a whole 4x4x8 slice. The times are simulated.
256 devices in a mesh: req: 32 (over y, x, z_hi), tp: 8 (over z_lo, core).
Axes of the slice: x: 4, y: 4, z: 8 (z_hi: 2, z_lo: 4; z = z_hi * 4 + z_lo), core: 2. Of those that a mesh axis runs over, the one named last changes fastest.
Arguments:
- residual: bfloat16 [8192, 2304], P('req'), may hold values from -58 to 58
- context: bfloat16 [8192, 2304], P('req', 'tp'), may hold values from -6 to 6
- attention_output_weight: bfloat16 [2304, 2304], P('tp'), may hold values from -0.1875 to 0.1875
- adapter_down_maps: bfloat16 [64, 2304, 16], P('req', 'tp'), may hold values from -0.125 to 0.125
- adapter_up_maps: bfloat16 [64, 16, 2304], P('req'), may hold values from -1.5 to 1.5
- adapter_storage_row: int32 [64], replicated, may hold values from 0 to 63, each once
- active_adapters: int32 [16], replicated, may hold values from 0 to 63, as said below
- request_token_length: int32 [32, 4], P('req'), may hold values from 1 to 128, 256 in all within a row
- request_adapter_entry: int32 [32, 4], P('req'), may hold values from 0 to 15
- expert_norm_gain: bfloat16 [2304], replicated, may hold values from 0.099609375 to 1.8984375
- router_projection: bfloat16 [2304, 8], replicated, may hold values from -0.125 to 0.125
- expert_choice_pairs: int32 [8192, 2], P('req'), may hold values from 0 to 7, all different within a row; in each aligned block of 256 rows (0 to 255, 256 to 511, ...) at most 80 rows name the same one
- expert_gate_weight: bfloat16 [32, 2304, 5760], P('req', None, 'tp'), as said below
- expert_up_weight: bfloat16 [32, 2304, 5760], P('req', None, 'tp'), as said below
- expert_down_weight: bfloat16 [32, 5760, 2304], P('req', 'tp'), as said below
Outputs:
- layer_out: bfloat16 [8192, 2304], P('req', 'tp')
Inputs may be any that keep to these rules, and one draw needn't show every extreme that they name: `active_adapters`: 16 different adapter numbers, 0 and 63 among them. `adapter_storage_row`: every stored row appears once. `request_token_length`: each group's lengths sum to 256; the longest request of a group has exactly half of 256 tokens. `expert_choice_pairs`: each row names two different experts; within the 256 rows of one group no expert is named by more than 80 rows, a bound that some block reaches. `expert_gate_weight`: the 4 holders c * 8 + e of expert e hold the same weights. `expert_up_weight`: the 4 holders c * 8 + e of expert e hold the same weights. `expert_down_weight`: the 4 holders c * 8 + e of expert e hold the same weights.
All inputs are finite; a program needn't handle non-finite values.
Results may differ from a plain program's by a relative error of at most 0.0095.
Values may be sent and summed in bfloat16 or wider, within the bound.
A program may use at most 128 MiB of HBM per device.

v0:
```python
import jax
import jax.numpy as jnp
from jax import lax
from jax.sharding import PartitionSpec as P

CAP = 80


NORM_EPS = 1e-05


def adapter_onehot(request_token_length, request_adapter_entry, active_count, token_count):
    bounds = jnp.cumsum(request_token_length[0])
    position = jnp.arange(token_count, dtype=jnp.int32)
    segment = jnp.sum((position[:, None] >= bounds[None, :]).astype(jnp.int32), axis=1)
    slot_range = jnp.arange(request_token_length.shape[1], dtype=jnp.int32)
    segment_hot = (segment[:, None] == slot_range[None, :]).astype(jnp.int32)
    token_pick = jnp.sum(segment_hot * request_adapter_entry[0][None, :], axis=1)
    return token_pick[:, None] == jnp.arange(active_count, dtype=jnp.int32)[None, :]


def route_tables(expert_choice_pairs, expert_count, capacity):
    expert_ids = jnp.arange(expert_count, dtype=jnp.int32)
    first_hit = expert_choice_pairs[None, :, 0] == expert_ids[:, None]
    second_hit = expert_choice_pairs[None, :, 1] == expert_ids[:, None]
    chosen = first_hit | second_hit
    slot_of = jnp.cumsum(chosen.astype(jnp.int32), axis=1) - 1
    slot_range = jnp.arange(capacity, dtype=jnp.int32)
    placement = chosen[:, None, :] & (slot_of[:, None, :] == slot_range[None, :, None])
    return (placement, first_hit, second_hit)


def on_device(
    residual,
    context,
    attention_output_weight,
    adapter_down_maps,
    adapter_up_maps,
    adapter_storage_row,
    active_adapters,
    request_token_length,
    request_adapter_entry,
    expert_norm_gain,
    router_projection,
    expert_choice_pairs,
    expert_gate_weight,
    expert_up_weight,
    expert_down_weight,
):
    token_count = residual.shape[0]
    hidden_width = residual.shape[1]
    active_count = active_adapters.shape[0]
    adapter_rank_size = adapter_down_maps.shape[2]
    stored_rows = adapter_storage_row[active_adapters]
    all_down, all_up = (
        lax.all_gather(adapter_down_maps, "req", axis=0, tiled=True),
        lax.all_gather(adapter_up_maps, "req", axis=0, tiled=True),
    )
    active_down = all_down[stored_rows]
    active_up = all_up[stored_rows]
    adapter_indicator = adapter_onehot(
        request_token_length, request_adapter_entry, active_count, token_count
    )
    down_joined = jnp.transpose(active_down, (1, 0, 2)).reshape(
        context.shape[1], active_count * adapter_rank_size
    )
    up_joined = active_up.reshape(active_count * adapter_rank_size, hidden_width)
    low_all = jnp.dot(context, down_joined, preferred_element_type=jnp.float32)
    reduced_mask = jnp.repeat(adapter_indicator, adapter_rank_size, axis=1)
    low_rank = jnp.where(reduced_mask, low_all, 0.0).astype(jnp.bfloat16)
    head_part = jnp.dot(
        context, attention_output_weight, preferred_element_type=jnp.float32
    ) + jnp.dot(low_rank, up_joined, preferred_element_type=jnp.float32)
    share_width = hidden_width // lax.axis_size("tp")
    share_start = lax.axis_index("tp") * share_width
    gain_all = expert_norm_gain.astype(jnp.float32)
    head_sum = lax.psum(head_part.astype(jnp.bfloat16), "tp").astype(jnp.float32)
    blended_rows = residual.astype(jnp.float32) + head_sum
    mean_square = jnp.mean(blended_rows * blended_rows, axis=1, keepdims=True)
    normed = (blended_rows * lax.rsqrt(mean_square + NORM_EPS) * gain_all).astype(jnp.bfloat16)
    mixed_share = lax.dynamic_slice_in_dim(blended_rows, share_start, share_width, 1)
    logits = jnp.dot(normed, router_projection, preferred_element_type=jnp.float32)
    expert_count = router_projection.shape[1]
    expert_range = jnp.arange(expert_count, dtype=jnp.int32)
    logit_first = jnp.sum(
        jnp.where(expert_choice_pairs[:, 0:1] == expert_range[None, :], logits, 0.0), axis=1
    )
    logit_second = jnp.sum(
        jnp.where(expert_choice_pairs[:, 1:2] == expert_range[None, :], logits, 0.0), axis=1
    )
    weight_first = 1.0 / (1.0 + jnp.exp(logit_second - logit_first))
    weight_second = 1.0 / (1.0 + jnp.exp(logit_first - logit_second))
    copy_count = lax.axis_size("req") // expert_count
    quota_slots = CAP // copy_count
    placement, first_hit, second_hit = route_tables(expert_choice_pairs, expert_count, CAP)
    holder_place = jnp.transpose(
        placement.reshape(expert_count, copy_count, quota_slots, token_count), (1, 0, 2, 3)
    ).reshape(copy_count * expert_count, quota_slots, token_count)
    send_rows = jnp.einsum(
        "hqt,td->hqd", holder_place.astype(jnp.bfloat16), normed, preferred_element_type=jnp.float32
    ).astype(jnp.bfloat16)
    gate_local = expert_gate_weight[0]
    up_local = expert_up_weight[0]
    down_local = expert_down_weight[0]
    rows_in = lax.all_to_all(send_rows, "req", split_axis=0, concat_axis=0, tiled=True)
    gate_value = jnp.einsum("nqd,df->nqf", rows_in, gate_local, preferred_element_type=jnp.float32)
    up_value = jnp.einsum("nqd,df->nqf", rows_in, up_local, preferred_element_type=jnp.float32)
    hidden = (jax.nn.silu(gate_value) * up_value).astype(jnp.bfloat16)
    partial_value = jnp.einsum(
        "nqf,fd->nqd", hidden, down_local, preferred_element_type=jnp.float32
    )
    token_weight = jnp.where(first_hit, weight_first[None, :], 0.0) + jnp.where(
        second_hit, weight_second[None, :], 0.0
    )
    holder_weight = jnp.tile(token_weight, (copy_count, 1))
    scaled_place = holder_place.astype(jnp.float32) * holder_weight[:, None, :]
    returned = lax.all_to_all(
        partial_value.astype(jnp.bfloat16), "req", split_axis=0, concat_axis=0, tiled=True
    )
    contribution = jnp.einsum(
        "hqt,hqd->td",
        scaled_place,
        returned.astype(jnp.float32),
        precision=lax.Precision.HIGHEST,
        preferred_element_type=jnp.float32,
    )
    moe_share = lax.psum_scatter(
        contribution.astype(jnp.bfloat16), "tp", scatter_dimension=1, tiled=True
    ).astype(jnp.float32)
    return (mixed_share + moe_share).astype(jnp.bfloat16)


def solution(mesh):
    return jax.shard_map(
        on_device,
        mesh=mesh,
        in_specs=(
            P("req", None),
            P("req", "tp"),
            P("tp", None),
            P("req", "tp", None),
            P("req", None, None),
            P(),
            P(),
            P("req", None),
            P("req", None),
            P(),
            P(),
            P("req", None),
            P("req", None, "tp"),
            P("req", None, "tp"),
            P("req", "tp", None),
        ),
        out_specs=P("req", "tp"),
        check_vma=False,
    )
```

profile of v0, /device:TPU:1, one launch (start us, length us, event | category | flops | bytes accessed | tf_op | source)
XLA Modules:
  0.0 503.3 jit_solution(13145580559629970987)
XLA Ops:
  8.2 1.3 reduce-window.18
  11.8 1.3 gather_fusion
  13.2 130.7 %all_gather.6 = bf16[64,288,16]{1,2,0:T(8,128)(2,1)} all-gather(bf16[2,288,16]{1,2,0:T(8,128)(2,1)} %param.18), channel_id=1, replica_groups=mesh['req'=32,'tp'=8] {'req'}, dimensions={0}, use_global_device_ids=true | all-gather | bytes 608256 | tf_op jit(solution)/shard_map/all_gather | solution.py:56
  143.9 1.7 gather_fusion.1
  147.1 3.6 fusion.42
  150.8 4.0 gather_fusion.2
  155.4 3.9 fusion.1
  159.6 82.0 %all-reduce.2.cloned.1.call-done = bf16[256,2304]{1,0:T(8,128)(2,1)} async-done(((bf16[256,2304]{1,0:T(8,128)(2,1)}), bf16[256,2304]{1,0:T(8,128)(2,1)}) %all-reduce.2.cloned.1.call-update) | async-done | bytes 1179664 | tf_op jit(solution)/shard_map/psum | solution.py:77
  241.5 3.6 convert_add_fusion
  245.1 1.2 convolution_convert_fusion.1
  246.3 1.6 copy.30
  247.9 93.1 %all_to_all.10 = bf16[32,20,2304]{2,1,0:T(8,128)(2,1)S(1)} all-to-all(bf16[32,20,2304]{2,1,0:T(8,128)(2,1)S(1)} %copy.30), channel_id=1, replica_groups=mesh['req'=32,'tp'=8] {'req'}, dimensions={0} | all-to-all | bytes 5898240 | tf_op jit(solution)/shard_map/all_to_all | solution.py:105
  341.0 1.8 copy-done.3
  342.9 3.8 fusion.6
  346.6 11.1 %convolution_convert_fusion = bf16[32,20,2304]{2,0,1:T(8,128)(2,1)} fusion(bf16[1,720,2304]{2,1,0:T(8,128)(2,1)S(1)} %copy-done, f32[32,20,720]{2,0,1:T(8,128)} %fusion.6, bf16[1,2304,720]{1,2,0:T(8,128)(2,1)} %param.28, bf16[32,20,2304]{2,1,0:T(8,128)(2,1)} %copy-done.3), kind=kOutput, calls=%fused_computation.3 | convolution fusion | flops 4250972160 | bytes 14376960 | tf_op jit(solution)/shard_map/nqf,fd->nqd/dot_general | solution.py:109
  357.7 5.3 %copy.33 = bf16[32,20,2304]{2,1,0:T(8,128)(2,1)} copy(bf16[32,20,2304]{2,0,1:T(8,128)(2,1)} %convolution_convert_fusion) | data formatting | bytes 5898240 | tf_op jit(solution)/shard_map/convert_element_type | solution.py:118
  363.0 6.3 %all-to-all-start.1 = ((bf16[32,20,2304]{2,1,0:T(8,128)(2,1)}), bf16[32,20,2304]{2,1,0:T(8,128)(2,1)}, u32[]{:S(2)}, u32[]{:S(2)}) async-start(bf16[32,20,2304]{2,1,0:T(8,128)(2,1)} %copy.33), calls=%async_computation.1 | async-start | bytes 7077888 | tf_op jit(solution)/shard_map/all_to_all | solution.py:117
  369.6 2.2 select_reduce_fusion.1
  371.8 74.6 %all-to-all-done.1 = bf16[32,20,2304]{2,1,0:T(8,128)(2,1)} async-done(((bf16[32,20,2304]{2,1,0:T(8,128)(2,1)}), bf16[32,20,2304]{2,1,0:T(8,128)(2,1)}, u32[]{:S(2)}, u32[]{:S(2)}) %all-to-all-start.1) | async-done | bytes 2949152 | tf_op jit(solution)/shard_map/all_to_all | solution.py:117
  446.4 6.8 %fusion.2 = bf16[2304,256]{1,0:T(8,128)(2,1)} fusion(bf16[32,20,2304]{2,1,0:T(8,128)(2,1)} %all-to-all-done.1, f32[32,256]{1,0:T(8,128)S(1)} %broadcast_bitcast_fusion, s32[32,20]{0,1:T(8,128)S(1)} %copy.29, s32[32,256]{1,0:T(8,128)S(1)} %broadcast_bitcast_fusion.1, pred[32,256]{1,0:T(8,128)(4,1)S(1)} %broadcast_bitcast_fusion.2), kind=kOutput, calls=%fused_computation.9 | convolution fusion | flops 4530929664 | bytes 4205056 | tf_op jit(solution)/shard_map/hqt,hqd->td/dot_general | solution.py:120
  453.2 38.9 %reduce-scatter.4.cloned.1.call-done = bf16[288,256]{1,0:T(8,128)(2,1)} async-done(((bf16[2304,256]{1,0:T(8,128)(2,1)}), bf16[288,256]{1,0:T(8,128)(2,1)}) %reduce-scatter.4.cloned.1.call-update) | async-done | bytes 147472
  492.1 1.1 copy.38
  493.2 1.9 add_convert_fusion
  495.1 1.7 copy.36
  (47 shorter events, 6.6 us)
Async XLA Ops:
  6.5 340.1 %copy-start = (bf16[1,720,2304]{2,1,0:T(8,128)(2,1)S(1)}, bf16[1,720,2304]{2,1,0:T(8,128)(2,1)}, u32[]{:S(2)}) copy-start(bf16[1,720,2304]{2,1,0:T(8,128)(2,1)} %param.29) | copy-start | bytes 9953284
  6.5 144.2 %all-gather.2.cloned.1.call-start = ((), (), s32[]{:S(2)}) async-start(), calls=%async_computation.3 | async-start | bytes 4866048 | tf_op jit(solution)/shard_map/all_gather | solution.py:57
  7.3 234.3 %all-reduce.2.cloned.1.call-start = ((), (), s32[]{:S(2)}) async-start(), calls=%async_computation.4 | async-start | bytes 2359296 | tf_op jit(solution)/shard_map/psum | solution.py:77
  11.2 139.6 %copy-start.4 = (s32[8,3]{0,1:T(4,128)}, s32[8,3]{0,1:T(4,128)S(1)}, u32[]{:S(2)}) copy-start(s32[8,3]{0,1:T(4,128)S(1)} %reduce-window.20) | copy-start | bytes 292
  155.4 4.1 slice-start
  241.5 3.6 copy-start.1
  241.5 3.6 copy-start.2
  247.9 94.9 %copy-start.5 = (bf16[1,2304,720]{1,2,0:T(8,128)(2,1)S(1)}, bf16[1,2304,720]{1,2,0:T(8,128)(2,1)}, u32[]{:S(2)}) copy-start(bf16[1,2304,720]{1,2,0:T(8,128)(2,1)} %param.27) | copy-start | bytes 9953284
  341.0 1.8 copy-start.3
  363.0 6.5 %copy-start.6 = (bf16[2304,8]{0,1:T(8,128)(2,1)S(1)}, bf16[2304,8]{0,1:T(8,128)(2,1)}, u32[]{:S(2)}) copy-start(bf16[2304,8]{0,1:T(8,128)(2,1)} %param.25) | copy-start | bytes 110596
  363.0 83.4 %all-to-all-start.1 = ((bf16[32,20,2304]{2,1,0:T(8,128)(2,1)}), bf16[32,20,2304]{2,1,0:T(8,128)(2,1)}, u32[]{:S(2)}, u32[]{:S(2)}) async-start(bf16[32,20,2304]{2,1,0:T(8,128)(2,1)} %copy.33), calls=%async_computation.1 | async-start | bytes 7077888 | tf_op jit(solution)/shard_map/all_to_all | solution.py:117
  369.3 122.8 %reduce-scatter.4.cloned.1.call-start = ((), (), s32[]{:S(2)}) async-start(), calls=%async_computation.5 | async-start | bytes 1327104
Sparse Core Ops, SparseCore 0:
  10.8 130.5 all-gather.1
  159.5 82.0 all-reduce.1
  453.4 38.6 reduce-scatter.3
where the time goes:
time: 506 us; the launch traced here: 503 us
  blocking collectives  224 us (44%)
  waiting for transfers between devices  196 us (39%)
  matrix products  32.6 us (6%)
  local copies, waits for them, and re-layouts  20.3 us (4%)
  between operations  13.2 us (3%)
  other arithmetic  10.6 us (2%)
  starting transfers between devices  6.56 us (1%)
    all_gather x1, blocking collectives, on_device(): lax.all_gather(adapter_down_maps, 'req', axis=0, tiled=True)  131 us
    all_to_all x1, blocking collectives, on_device(): lax.all_to_all(send_rows, 'req', split_axis=0, concat_axis=0, tiled=True)  93.1 us
    psum x1, waiting for transfers between devices, on_device(): lax.psum(head_part.astype(jnp.bfloat16), 'tp').astype(jnp.float32)  82 us
    all_to_all x1, waiting for transfers between devices, on_device(): lax.all_to_all(partial_value.astype(jnp.bfloat16), 'req', split_axis=0, c...  74.6 us
    unnamed x4, waiting for transfers between devices  39.6 us
    dot_general x1, matrix products, on_device(): jnp.einsum('nqf,fd->nqd', hidden, down_local, preferred_element_type=jnp....  11.1 us
  transfers between devices with their start and end apart: 4, of which 3 were waited for; matrix products, arithmetic and copies ran while one was open for 3% of the time, Pallas kernels for 0%

commit v1 on v0

v1 whole, which is shorter than its diff:
```python
import jax
import jax.numpy as jnp
from jax import lax
from jax.sharding import Mesh
from jax.sharding import PartitionSpec as P

CAP = 80


NORM_EPS = 1e-05

REQ = ("ry", "rxz")


def segment_onehot(request_token_length, token_count):
    bounds = jnp.cumsum(request_token_length[0])
    position = jnp.arange(token_count, dtype=jnp.int32)
    segment = jnp.sum((position[:, None] >= bounds[None, :]).astype(jnp.int32), axis=1)
    slot_range = jnp.arange(request_token_length.shape[1], dtype=jnp.int32)
    return segment[:, None] == slot_range[None, :]


def route_tables(expert_choice_pairs, expert_count, capacity):
    expert_ids = jnp.arange(expert_count, dtype=jnp.int32)
    first_hit = expert_choice_pairs[None, :, 0] == expert_ids[:, None]
    second_hit = expert_choice_pairs[None, :, 1] == expert_ids[:, None]
    chosen = first_hit | second_hit
    slot_of = jnp.cumsum(chosen.astype(jnp.int32), axis=1) - 1
    slot_range = jnp.arange(capacity, dtype=jnp.int32)
    placement = chosen[:, None, :] & (slot_of[:, None, :] == slot_range[None, :, None])
    return (placement, first_hit, second_hit)


def on_device(
    residual,
    context,
    attention_output_weight,
    adapter_down_maps,
    adapter_up_maps,
    adapter_storage_row,
    active_adapters,
    request_token_length,
    request_adapter_entry,
    expert_norm_gain,
    router_projection,
    expert_choice_pairs,
    expert_gate_weight,
    expert_up_weight,
    expert_down_weight,
):
    token_count = residual.shape[0]
    hidden_width = residual.shape[1]
    feature_share = context.shape[1]
    local_rows = adapter_down_maps.shape[0]
    adapter_rank_size = adapter_down_maps.shape[2]
    request_count = request_token_length.shape[1]
    share_width = hidden_width // lax.axis_size("tp")
    share_start = lax.axis_index("tp") * share_width

    up_slice = lax.dynamic_slice_in_dim(adapter_up_maps, share_start, share_width, 2)
    packed = jnp.concatenate(
        [
            adapter_down_maps.reshape(local_rows, feature_share * adapter_rank_size),
            up_slice.reshape(local_rows, adapter_rank_size * share_width),
        ],
        axis=1,
    )
    all_packed = lax.all_gather(packed, REQ, axis=0, tiled=True)
    request_rows = adapter_storage_row[active_adapters[request_adapter_entry[0]]]
    picked = all_packed[request_rows]
    down_req = picked[:, : feature_share * adapter_rank_size].reshape(
        request_count, feature_share, adapter_rank_size
    )
    up_req = picked[:, feature_share * adapter_rank_size :].reshape(
        request_count * adapter_rank_size, share_width
    )
    down_joined = jnp.transpose(down_req, (1, 0, 2)).reshape(
        feature_share, request_count * adapter_rank_size
    )
    segment_hot = segment_onehot(request_token_length, token_count)
    low_all = jnp.dot(context, down_joined, preferred_element_type=jnp.float32)
    reduced_mask = jnp.repeat(segment_hot, adapter_rank_size, axis=1)
    low_part = jnp.where(reduced_mask, low_all, 0.0)
    low_total = lax.psum(low_part, "tp").astype(jnp.bfloat16)
    lora_share = jnp.dot(low_total, up_req, preferred_element_type=jnp.float32)

    base = jnp.dot(context, attention_output_weight, preferred_element_type=jnp.float32)
    base_share = lax.dynamic_slice_in_dim(base, share_start, share_width, 1)
    head_part = lax.dynamic_update_slice_in_dim(base, base_share + lora_share, share_start, 1)
    gain_all = expert_norm_gain.astype(jnp.float32)
    head_sum = lax.psum(head_part.astype(jnp.bfloat16), "tp").astype(jnp.float32)
    blended_rows = residual.astype(jnp.float32) + head_sum
    mean_square = jnp.mean(blended_rows * blended_rows, axis=1, keepdims=True)
    normed = (blended_rows * lax.rsqrt(mean_square + NORM_EPS) * gain_all).astype(jnp.bfloat16)
    mixed_share = lax.dynamic_slice_in_dim(blended_rows, share_start, share_width, 1)
    logits = jnp.dot(normed, router_projection, preferred_element_type=jnp.float32)
    expert_count = router_projection.shape[1]
    expert_range = jnp.arange(expert_count, dtype=jnp.int32)
    logit_first = jnp.sum(
        jnp.where(expert_choice_pairs[:, 0:1] == expert_range[None, :], logits, 0.0), axis=1
    )
    logit_second = jnp.sum(
        jnp.where(expert_choice_pairs[:, 1:2] == expert_range[None, :], logits, 0.0), axis=1
    )
    weight_first = 1.0 / (1.0 + jnp.exp(logit_second - logit_first))
    weight_second = 1.0 / (1.0 + jnp.exp(logit_first - logit_second))

    placement, first_hit, second_hit = route_tables(expert_choice_pairs, expert_count, CAP)
    send_rows = jnp.einsum(
        "est,td->esd", placement.astype(jnp.bfloat16), normed, preferred_element_type=jnp.float32
    ).astype(jnp.bfloat16)
    rows_in = lax.all_to_all(send_rows, "rxz", split_axis=0, concat_axis=0, tiled=True)
    rows_flat = rows_in.reshape(expert_count * CAP, hidden_width)
    gate_value = jnp.dot(rows_flat, expert_gate_weight[0], preferred_element_type=jnp.float32)
    up_value = jnp.dot(rows_flat, expert_up_weight[0], preferred_element_type=jnp.float32)
    hidden = (jax.nn.silu(gate_value) * up_value).astype(jnp.bfloat16)
    partial_value = jnp.dot(hidden, expert_down_weight[0], preferred_element_type=jnp.float32)
    returned = lax.all_to_all(
        partial_value.astype(jnp.bfloat16).reshape(expert_count, CAP, hidden_width),
        "rxz",
        split_axis=0,
        concat_axis=0,
        tiled=True,
    )
    token_weight = jnp.where(first_hit, weight_first[None, :], 0.0) + jnp.where(
        second_hit, weight_second[None, :], 0.0
    )
    scaled_place = placement.astype(jnp.float32) * token_weight[:, None, :]
    contribution = jnp.einsum(
        "est,esd->td",
        scaled_place,
        returned.astype(jnp.float32),
        precision=lax.Precision.HIGHEST,
        preferred_element_type=jnp.float32,
    )
    moe_share = lax.psum_scatter(
        contribution.astype(jnp.bfloat16), "tp", scatter_dimension=1, tiled=True
    ).astype(jnp.float32)
    return (mixed_share + moe_share).astype(jnp.bfloat16)


def solution(mesh):
    req_size = mesh.shape["req"]
    plane = 8
    split_mesh = Mesh(
        mesh.devices.reshape(req_size // plane, plane, mesh.shape["tp"]), ("ry", "rxz", "tp")
    )
    return jax.shard_map(
        on_device,
        mesh=split_mesh,
        in_specs=(
            P(REQ, None),
            P(REQ, "tp"),
            P("tp", None),
            P(REQ, "tp", None),
            P(REQ, None, None),
            P(),
            P(),
            P(REQ, None),
            P(REQ, None),
            P(),
            P(),
            P(REQ, None),
            P(REQ, None, "tp"),
            P(REQ, None, "tp"),
            P(REQ, "tp", None),
        ),
        out_specs=P(REQ, "tp"),
        check_vma=False,
    )
```

time: 506 us -> 435 us (0.86)
  blocking collectives: 224 us -> 103 us
  waiting for transfers between devices: 196 us -> 242 us
    all_gather x1 -> x0, blocking collectives: 131 us -> none  [on_device(): lax.all_gather(adapter_down_maps, 'req', axis=0, tiled=True)]
    all_gather x1, waiting for transfers between devices: 0.01 us -> 76 us  [on_device(): all_packed = lax.all_gather(packed, REQ, axis=0, tiled=True)]
    psum x0 -> x1, blocking collectives: none -> 27 us  [on_device(): low_total = lax.psum(low_part, 'tp').astype(jnp.bfloat16)]
    all_to_all x1, blocking collectives: 93.1 us -> 75.7 us  [on_device(): lax.all_to_all(send_rows, 'rxz', split_axis=0, concat_axis=0, tiled=True)]
    psum x1, waiting for transfers between devices: 82 us -> 68.8 us  [on_device(): lax.psum(head_part.astype(jnp.bfloat16), 'tp').astype(jnp.float32)]
    all_to_all x1, waiting for transfers between devices: 74.6 us -> 62.3 us  [on_device(): lax.all_to_all(partial_value.astype(jnp.bfloat16).reshape(expert_count, C...]
    convert_element_type x2 -> x0, local copies, waits for them, and re-layouts: 6.92 us -> none  [the longest x1 5.29 us: on_device(): partial_value.astype(jnp.bfloat16)]
    dot_general x5 -> x6, matrix products: 26.7 us -> 29.1 us  [the longest x1 14.5 us: on_device(): jnp.dot(hidden, expert_down_weight[0], preferred_element_type=jnp.float32)]
  transfers between devices with their start and end apart: 4 -> 4, of which waited for: 3 -> 4; matrix products, arithmetic and copies ran while one was open for 3% -> 3% of each run, Pallas kernels for 0% -> 0%
where the time goes in v1:
time: 435 us; the launch traced here: 432 us
  waiting for transfers between devices  242 us (56%)
  blocking collectives  103 us (24%)
  matrix products  34.9 us (8%)
  local copies, waits for them, and re-layouts  23.2 us (5%)
  between operations  13.2 us (3%)
  other arithmetic  11.3 us (3%)
  starting transfers between devices  5.08 us (1%)
    all_gather x1, waiting for transfers between devices, on_device(): all_packed = lax.all_gather(packed, REQ, axis=0, tiled=True)  76 us
    all_to_all x1, blocking collectives, on_device(): lax.all_to_all(send_rows, 'rxz', split_axis=0, concat_axis=0, tiled=True)  75.7 us
    psum x1, waiting for transfers between devices, on_device(): lax.psum(head_part.astype(jnp.bfloat16), 'tp').astype(jnp.float32)  68.8 us
    all_to_all x1, waiting for transfers between devices, on_device(): lax.all_to_all(partial_value.astype(jnp.bfloat16).reshape(expert_count, C...  62.3 us
    unnamed x4, waiting for transfers between devices  34.8 us
    psum x1, blocking collectives, on_device(): low_total = lax.psum(low_part, 'tp').astype(jnp.bfloat16)  27 us
    dot_general x1, matrix products, on_device(): jnp.dot(hidden, expert_down_weight[0], preferred_element_type=jnp.float32)  14.5 us
  transfers between devices with their start and end apart: 4, of which 4 were waited for; matrix products, arithmetic and copies ran while one was open for 3% of the time, Pallas kernels for 0%

profile of v1, /device:TPU:1, one launch (start us, length us, event | category | flops | bytes accessed | tf_op | source)
XLA Modules:
  0.0 432.4 jit_solution(16234100951384589022)
XLA Ops:
  13.6 3.6 fusion.35
  17.2 76.0 %all-gather.3.cloned.1.call-done = bf16[32,2,9216]{2,1,0:T(2,128)(2,1)} async-done(((bf16[1,2,9216]{2,1,0:T(2,128)(2,1)}), bf16[32,2,9216]{2,1,0:T(2,128)(2,1)}) %all-gather.3.cloned.1.call-update) | async-done | bytes 1179664 | tf_op jit(solution)/shard_map/all_gather | solution.py:68
  93.2 2.3 reshape.300
  95.6 2.1 gather_fusion.2
  98.3 1.5 reshape.271
  99.8 1.7 reshape.269
  101.6 1.7 copy.30
  104.3 27.0 %psum.14 = bf16[256,64]{0,1:T(8,128)(2,1)S(1)} all-reduce(f32[256,64]{0,1:T(8,128)S(1)} %fusion.10), channel_id=1, replica_groups=mesh['ry'=4,'rxz'=8,'tp'=8] {'tp'}, use_global_device_ids=true, to_apply=%region_2.3 | all-reduce | flops 16384 | bytes 98304 | tf_op jit(solution)/shard_map/psum | solution.py:84
  131.3 2.1 convolution_add_fusion
  133.4 3.8 dynamic_update_slice.3
  137.2 2.8 convert_element_type.49
  141.0 68.8 %all-reduce.2.cloned.1.call-done = bf16[256,2304]{1,0:T(8,128)(2,1)} async-done(((bf16[256,2304]{1,0:T(8,128)(2,1)}), bf16[256,2304]{1,0:T(8,128)(2,1)}) %all-reduce.2.cloned.1.call-update) | async-done | bytes 1179664 | tf_op jit(solution)/shard_map/psum | solution.py:91
  209.8 3.6 convert_add_fusion
  214.5 75.7 %all_to_all.10 = bf16[8,80,2304]{2,1,0:T(8,128)(2,1)S(1)} all-to-all(bf16[8,80,2304]{2,1,0:T(8,128)(2,1)S(1)} %convolution_convert_fusion.1), channel_id=1, replica_groups=mesh['ry'=4,'rxz'=8,'tp'=8] {'rxz'}, dimensions={0} | all-to-all | bytes 5898240 | tf_op jit(solution)/shard_map/all_to_all | solution.py:112
  290.2 1.6 copy-done.3
  291.8 4.0 fusion.5
  295.8 14.5 %convolution_convert_fusion = bf16[640,2304]{1,0:T(8,128)(2,1)} fusion(bf16[1,720,2304]{2,1,0:T(8,128)(2,1)S(1)} %copy-done, f32[640,720]{0,1:T(8,128)} %fusion.5, bf16[640,2304]{1,0:T(8,128)(2,1)} %bitcast.68, bf16[1,2304,720]{1,2,0:T(8,128)(2,1)} %param.28), kind=kOutput, calls=%fused_computation.3 | convolution fusion | flops 4250972160 | bytes 14376960 | tf_op jit(solution)/shard_map/dot_general | solution.py:117
  310.3 4.8 %all-to-all-start.1 = ((bf16[8,80,2304]{2,1,0:T(8,128)(2,1)}), bf16[8,80,2304]{2,1,0:T(8,128)(2,1)}, u32[]{:S(2)}, u32[]{:S(2)}) async-start(bf16[8,80,2304]{2,1,0:T(8,128)(2,1)} %bitcast.66), calls=%async_computation.1 | async-start | bytes 5898240 | tf_op jit(solution)/shard_map/all_to_all | solution.py:118
  315.4 2.2 select_reduce_fusion.1
  317.6 62.3 %all-to-all-done.1 = bf16[8,80,2304]{2,1,0:T(8,128)(2,1)} async-done(((bf16[8,80,2304]{2,1,0:T(8,128)(2,1)}), bf16[8,80,2304]{2,1,0:T(8,128)(2,1)}, u32[]{:S(2)}, u32[]{:S(2)}) %all-to-all-start.1) | async-done | bytes 2949152 | tf_op jit(solution)/shard_map/all_to_all | solution.py:118
  380.0 6.4 %fusion.1 = bf16[2304,256]{1,0:T(8,128)(2,1)} fusion(bf16[8,80,2304]{2,1,0:T(8,128)(2,1)} %all-to-all-done.1, f32[8,256]{1,0:T(8,128)S(1)} %select_add_fusion, s32[8,256]{1,0:T(8,128)S(1)} %add_bitcast_fusion, pred[8,256]{1,0:T(8,128)(4,1)S(1)} %fusion.24), kind=kOutput, calls=%fused_computation.7 | convolution fusion | flops 4530929664 | bytes 4147200 | tf_op jit(solution)/shard_map/est,esd->td/dot_general | solution.py:129
  386.4 34.7 %reduce-scatter.4.cloned.1.call-done = bf16[288,256]{1,0:T(8,128)(2,1)} async-done(((bf16[2304,256]{1,0:T(8,128)(2,1)}), bf16[288,256]{1,0:T(8,128)(2,1)}) %reduce-scatter.4.cloned.1.call-update) | async-done | bytes 147472
  422.2 1.9 add_convert_fusion
  424.1 1.7 copy.33
  (56 shorter events, 12.2 us)
Async XLA Ops:
  6.5 289.3 %copy-start = (bf16[1,720,2304]{2,1,0:T(8,128)(2,1)S(1)}, bf16[1,720,2304]{2,1,0:T(8,128)(2,1)}, u32[]{:S(2)}) copy-start(bf16[1,720,2304]{2,1,0:T(8,128)(2,1)} %param.29) | copy-start | bytes 9953284
  6.5 86.7 %all-gather.3.cloned.1.call-start = ((), (), s32[]{:S(2)}) async-start(), calls=%async_computation.4 | async-start | bytes 1216512 | tf_op jit(solution)/shard_map/all_gather | solution.py:68
  9.4 200.4 %all-reduce.2.cloned.1.call-start = ((), (), s32[]{:S(2)}) async-start(), calls=%async_computation.3 | async-start | bytes 2359296 | tf_op jit(solution)/shard_map/psum | solution.py:91
  17.2 86.1 %copy-start.4 = (bf16[256,288]{0,1:T(8,128)(2,1)S(1)}, bf16[256,288]{0,1:T(8,128)(2,1)}, u32[]{:S(2)}) copy-start(bf16[256,288]{0,1:T(8,128)(2,1)} %param.16) | copy-start | bytes 442372
  137.2 2.8 copy-start.6
  137.2 3.7 copy-start.5
  209.8 3.6 copy-start.1
  209.8 3.6 copy-start.2
  214.5 77.3 %copy-start.7 = (bf16[1,2304,720]{1,2,0:T(8,128)(2,1)S(1)}, bf16[1,2304,720]{1,2,0:T(8,128)(2,1)}, u32[]{:S(2)}) copy-start(bf16[1,2304,720]{1,2,0:T(8,128)(2,1)} %param.27) | copy-start | bytes 9953284
  290.2 1.6 copy-start.3
  310.3 5.0 %copy-start.8 = (bf16[2304,8]{0,1:T(8,128)(2,1)S(1)}, bf16[2304,8]{0,1:T(8,128)(2,1)}, u32[]{:S(2)}) copy-start(bf16[2304,8]{0,1:T(8,128)(2,1)} %param.25) | copy-start | bytes 110596
  310.3 69.6 %all-to-all-start.1 = ((bf16[8,80,2304]{2,1,0:T(8,128)(2,1)}), bf16[8,80,2304]{2,1,0:T(8,128)(2,1)}, u32[]{:S(2)}, u32[]{:S(2)}) async-start(bf16[8,80,2304]{2,1,0:T(8,128)(2,1)} %bitcast.66), calls=%async_computation.1 | async-start | bytes 5898240 | tf_op jit(solution)/shard_map/all_to_all | solution.py:118
  315.1 106.1 %reduce-scatter.4.cloned.1.call-start = ((), (), s32[]{:S(2)}) async-start(), calls=%async_computation.5 | async-start | bytes 1327104
Sparse Core Ops, SparseCore 0:
  10.8 82.3 all-gather.2
  140.1 69.5 all-reduce.1
  386.5 34.5 reduce-scatter.3

commit v2 on v1

--- a/solution.py
+++ b/solution.py
@@ -10,6 +10,8 @@
 NORM_EPS = 1e-05
 
 REQ = ("ry", "rxz")
+TP = ("tz", "tc")
+PAIR = [(0, 1), (1, 0)]
 
 
 def segment_onehot(request_token_length, token_count):
@@ -29,6 +31,25 @@
     slot_range = jnp.arange(capacity, dtype=jnp.int32)
     placement = chosen[:, None, :] & (slot_of[:, None, :] == slot_range[None, :, None])
     return (placement, first_hit, second_hit)
+
+
+def pair_psum(value, share_width):
+    rows = value.shape[0]
+    chip_count = lax.axis_size("tz")
+    core = lax.axis_index("tc")
+    split = value.reshape(rows, chip_count, 2, share_width)
+    keep = lax.dynamic_index_in_dim(split, core, 2, keepdims=False)
+    give = lax.dynamic_index_in_dim(split, 1 - core, 2, keepdims=False)
+    got = lax.ppermute(give, "tc", PAIR)
+    pair = (keep.astype(jnp.float32) + got.astype(jnp.float32)).astype(value.dtype)
+    chips = lax.psum(pair, "tz")
+    other = lax.ppermute(chips, "tc", PAIR)
+    joined = jnp.where(
+        core == 0,
+        jnp.stack([chips, other], axis=2),
+        jnp.stack([other, chips], axis=2),
+    )
+    return joined.reshape(value.shape)
 
 
 def on_device(
@@ -54,8 +75,8 @@
     local_rows = adapter_down_maps.shape[0]
     adapter_rank_size = adapter_down_maps.shape[2]
     request_count = request_token_length.shape[1]
-    share_width = hidden_width // lax.axis_size("tp")
-    share_start = lax.axis_index("tp") * share_width
+    share_width = hidden_width // (lax.axis_size("tz") * 2)
+    share_start = (lax.axis_index("tz") * 2 + lax.axis_index("tc")) * share_width
 
     up_slice = lax.dynamic_slice_in_dim(adapter_up_maps, share_start, share_width, 2)
     packed = jnp.concatenate(
@@ -81,14 +102,14 @@
     low_all = jnp.dot(context, down_joined, preferred_element_type=jnp.float32)
     reduced_mask = jnp.repeat(segment_hot, adapter_rank_size, axis=1)
     low_part = jnp.where(reduced_mask, low_all, 0.0)
-    low_total = lax.psum(low_part, "tp").astype(jnp.bfloat16)
+    low_total = lax.psum(low_part, TP).astype(jnp.bfloat16)
     lora_share = jnp.dot(low_total, up_req, preferred_element_type=jnp.float32)
 
     base = jnp.dot(context, attention_output_weight, preferred_element_type=jnp.float32)
     base_share = lax.dynamic_slice_in_dim(base, share_start, share_width, 1)
     head_part = lax.dynamic_update_slice_in_dim(base, base_share + lora_share, share_start, 1)
     gain_all = expert_norm_gain.astype(jnp.float32)
-    head_sum = lax.psum(head_part.astype(jnp.bfloat16), "tp").astype(jnp.float32)
+    head_sum = pair_psum(head_part.astype(jnp.bfloat16), share_width).astype(jnp.float32)
     blended_rows = residual.astype(jnp.float32) + head_sum
     mean_square = jnp.mean(blended_rows * blended_rows, axis=1, keepdims=True)
     normed = (blended_rows * lax.rsqrt(mean_square + NORM_EPS) * gain_all).astype(jnp.bfloat16)
@@ -109,14 +130,31 @@
     send_rows = jnp.einsum(
         "est,td->esd", placement.astype(jnp.bfloat16), normed, preferred_element_type=jnp.float32
     ).astype(jnp.bfloat16)
-    rows_in = lax.all_to_all(send_rows, "rxz", split_axis=0, concat_axis=0, tiled=True)
+    send_halves = send_rows.reshape(expert_count, CAP, 2, hidden_width // 2)
+    core = lax.axis_index("tc")
+    own_half = lax.dynamic_index_in_dim(send_halves, core, 2, keepdims=False)
+    half_in = lax.all_to_all(own_half, "rxz", split_axis=0, concat_axis=0, tiled=True)
+    other_in = lax.ppermute(half_in, "tc", PAIR)
+    rows_in = jnp.where(
+        core == 0,
+        jnp.concatenate([half_in, other_in], axis=2),
+        jnp.concatenate([other_in, half_in], axis=2),
+    )
     rows_flat = rows_in.reshape(expert_count * CAP, hidden_width)
     gate_value = jnp.dot(rows_flat, expert_gate_weight[0], preferred_element_type=jnp.float32)
     up_value = jnp.dot(rows_flat, expert_up_weight[0], preferred_element_type=jnp.float32)
     hidden = (jax.nn.silu(gate_value) * up_value).astype(jnp.bfloat16)
     partial_value = jnp.dot(hidden, expert_down_weight[0], preferred_element_type=jnp.float32)
+    chip_count = lax.axis_size("tz")
+    partial_split = partial_value.astype(jnp.bfloat16).reshape(
+        expert_count * CAP, chip_count, 2, share_width
+    )
+    keep_part = lax.dynamic_index_in_dim(partial_split, core, 2, keepdims=False)
+    give_part = lax.dynamic_index_in_dim(partial_split, 1 - core, 2, keepdims=False)
+    got_part = lax.ppermute(give_part, "tc", PAIR)
+    pair_value = (keep_part.astype(jnp.float32) + got_part.astype(jnp.float32)).astype(jnp.bfloat16)
     returned = lax.all_to_all(
-        partial_value.astype(jnp.bfloat16).reshape(expert_count, CAP, hidden_width),
+        pair_value.reshape(expert_count, CAP, chip_count * share_width),
         "rxz",
         split_axis=0,
         concat_axis=0,
@@ -134,7 +172,7 @@
         preferred_element_type=jnp.float32,
     )
     moe_share = lax.psum_scatter(
-        contribution.astype(jnp.bfloat16), "tp", scatter_dimension=1, tiled=True
+        contribution.astype(jnp.bfloat16), "tz", scatter_dimension=1, tiled=True
     ).astype(jnp.float32)
     return (mixed_share + moe_share).astype(jnp.bfloat16)
 
@@ -143,16 +181,17 @@
     req_size = mesh.shape["req"]
     plane = 8
     split_mesh = Mesh(
-        mesh.devices.reshape(req_size // plane, plane, mesh.shape["tp"]), ("ry", "rxz", "tp")
+        mesh.devices.reshape(req_size // plane, plane, mesh.shape["tp"] // 2, 2),
+        ("ry", "rxz", "tz", "tc"),
     )
     return jax.shard_map(
         on_device,
         mesh=split_mesh,
         in_specs=(
             P(REQ, None),
-            P(REQ, "tp"),
-            P("tp", None),
-            P(REQ, "tp", None),
+            P(REQ, TP),
+            P(TP, None),
+            P(REQ, TP, None),
             P(REQ, None, None),
             P(),
             P(),
@@ -161,10 +200,10 @@
             P(),
             P(),
             P(REQ, None),
-            P(REQ, None, "tp"),
-            P(REQ, None, "tp"),
-            P(REQ, "tp", None),
+            P(REQ, None, TP),
+            P(REQ, None, TP),
+            P(REQ, TP, None),
         ),
-        out_specs=P(REQ, "tp"),
+        out_specs=P(REQ, TP),
         check_vma=False,
     )

time: 435 us -> 392 us (0.901)
  waiting for transfers between devices: 242 us -> 188 us
  blocking collectives: 103 us -> 64.1 us
  local copies, waits for them, and re-layouts: 23.2 us -> 57 us
  starting transfers between devices: 5.08 us -> 18.4 us
    all_to_all x1, waiting for transfers between devices: 62.3 us -> 21.4 us  [on_device(): lax.all_to_all(pair_value.reshape(expert_count, CAP, chip_count * share_w...]
    all_to_all x1, blocking collectives: 75.7 us -> 37 us  [on_device(): lax.all_to_all(own_half, 'rxz', split_axis=0, concat_axis=0, tiled=True)]
    reduce_scatter x0 -> x1, waiting for transfers between devices: none -> 38.4 us  [on_device(): lax.psum_scatter(contribution.astype(jnp.bfloat16), 'tz', scatter_dimensi...]
    unnamed x4 -> x3, waiting for transfers between devices: 34.8 us -> 0.05 us
    psum x1, waiting for transfers between devices: 68.8 us -> 44.2 us  [pair_psum(): chips = lax.psum(pair, 'tz')]
    convert_element_type x1 -> x4, local copies, waits for them, and re-layouts: 1.7 us -> 12.6 us  [the longest x1 5.48 us: on_device(): partial_value.astype(jnp.bfloat16)]
    reshape x0 -> x2, local copies, waits for them, and re-layouts: none -> 10.9 us  [the longest x1 6.66 us: on_device(): send_halves = send_rows.reshape(expert_count, CAP, 2, hidden_width // 2)]
    ppermute x0 -> x4, starting transfers between devices: none -> 8.27 us  [the longest x1 3.76 us: pair_psum(): got = lax.ppermute(give, 'tc', PAIR)]
  transfers between devices with their start and end apart: 4 -> 8, of which waited for: 4 -> 7; matrix products, arithmetic and copies ran while one was open for 3% -> 3% of each run, Pallas kernels for 0% -> 0%
where the time goes in v2:
time: 392 us; the launch traced here: 389 us
  waiting for transfers between devices  188 us (48%)
  blocking collectives  64.1 us (16%)
  local copies, waits for them, and re-layouts  57 us (15%)
  matrix products  35.1 us (9%)
  starting transfers between devices  18.4 us (5%)
  other arithmetic  13.7 us (3%)
  between operations  13.3 us (3%)
    all_gather x1, waiting for transfers between devices, on_device(): all_packed = lax.all_gather(packed, REQ, axis=0, tiled=True)  76 us
    psum x1, waiting for transfers between devices, pair_psum(): chips = lax.psum(pair, 'tz')  44.2 us
    reduce_scatter x1, waiting for transfers between devices, on_device(): lax.psum_scatter(contribution.astype(jnp.bfloat16), 'tz', scatter_dimensi...  38.4 us
    all_to_all x1, blocking collectives, on_device(): lax.all_to_all(own_half, 'rxz', split_axis=0, concat_axis=0, tiled=True)  37 us
    psum x1, blocking collectives, on_device(): low_total = lax.psum(low_part, TP).astype(jnp.bfloat16)  27 us
    all_to_all x1, waiting for transfers between devices, on_device(): lax.all_to_all(pair_value.reshape(expert_count, CAP, chip_count * share_w...  21.4 us
    dot_general x1, matrix products, on_device(): jnp.dot(hidden, expert_down_weight[0], preferred_element_type=jnp.float32)  15.4 us
    all_to_all x1, starting transfers between devices, on_device(): lax.all_to_all(pair_value.reshape(expert_count, CAP, chip_count * share_w...  9.79 us
  transfers between devices with their start and end apart: 8, of which 7 were waited for; matrix products, arithmetic and copies ran while one was open for 3% of the time, Pallas kernels for 0%

profile of v2, /device:TPU:1, one launch (start us, length us, event | category | flops | bytes accessed | tf_op | source)
XLA Modules:
  0.0 389.4 jit_solution(9884065459109537018)
XLA Ops:
  13.6 3.6 fusion.40
  17.2 76.0 %all-gather.3.cloned.1.call-done = bf16[32,2,9216]{2,1,0:T(2,128)(2,1)} async-done(((bf16[1,2,9216]{2,1,0:T(2,128)(2,1)}), bf16[32,2,9216]{2,1,0:T(2,128)(2,1)}) %all-gather.3.cloned.1.call-update) | async-done | bytes 1179664 | tf_op jit(solution)/shard_map/all_gather | solution.py:89
  104.3 27.0 %psum.14 = bf16[256,64]{0,1:T(8,128)(2,1)S(1)} all-reduce(f32[256,64]{0,1:T(8,128)S(1)} %fusion.12), channel_id=1, replica_groups=mesh['ry'=4,'rxz'=8,'tz'=4,'tc'=2] {'tz','tc'}, use_global_device_ids=true, to_apply=%region_2.3 | all-reduce | flops 16384 | bytes 98304 | tf_op jit(solution)/shard_map/psum | solution.py:105
  133.4 3.8 dynamic_update_slice.3
  137.2 2.8 convert_element_type.76
  144.3 3.8 collective-permute-start
  152.3 44.2 %all-reduce.2.cloned.1.call-done = bf16[256,4,288]{0,2,1:T(8,128)(2,1)} async-done(((bf16[256,4,288]{0,2,1:T(8,128)(2,1)}), bf16[256,4,288]{0,2,1:T(8,128)(2,1)}) %all-reduce.2.cloned.1.call-update) | async-done | bytes 589840 | tf_op jit(solution)/shard_map/psum | solution.py:45
  196.5 2.6 collective-permute-start.1
  200.0 2.4 copy.40
  207.6 2.7 convolution_convert_fusion.1
  210.3 6.7 %reshape.296 = bf16[8,80,2,1152]{3,2,1,0:T(2,128)(2,1)} reshape(bf16[8,80,2304]{2,1,0:T(8,128)(2,1)} %convolution_convert_fusion.1) | data formatting | bytes 5898240 | tf_op jit(solution)/shard_map/reshape | solution.py:133
  216.9 4.9 %constant_dynamic-slice_fusion = bf16[8,80,1,1152]{3,2,1,0:T(2,128)(2,1)S(1)} fusion(bf16[8,80,2,1152]{3,2,1,0:T(2,128)(2,1)} %reshape.296, s32[]{:T(128)S(6)} %select_n.99), kind=kLoop, calls=%fused_computation.65 | loop fusion | bytes 2949124 | tf_op jit(solution)/shard_map/jit(dynamic_index_in_dim)/dynamic_slice | solution.py:135
  222.0 37.0 %all_to_all.10 = bf16[8,80,1152]{2,1,0:T(8,128)(2,1)S(1)} all-to-all(bf16[8,80,1152]{2,1,0:T(8,128)(2,1)S(1)} %bitcast.81), channel_id=1, replica_groups=mesh['ry'=4,'rxz'=8,'tz'=4,'tc'=2] {'rxz'}, dimensions={0} | all-to-all | bytes 2949120 | tf_op jit(solution)/shard_map/all_to_all | solution.py:136
  260.5 2.9 collective-permute-done.2
  264.5 4.1 %fusion.3 = f32[640,720]{0,1:T(8,128)} fusion(bf16[1,2304,720]{1,2,0:T(8,128)(2,1)S(1)} %copy-done.9, bf16[640,1152]{1,0:T(8,128)(2,1)S(1)} %bitcast.98, bf16[640,1152]{1,0:T(8,128)(2,1)S(1)} %bitcast.84, pred[]{:T(512)S(6)} %eq.118), kind=kOutput, calls=%fused_computation.8 | convolution fusion | flops 2136637440 | bytes 8110081 | tf_op jit(solution)/shard_map/dot_general | solution.py:144
  268.7 15.4 %convolution_convert_fusion = bf16[640,2304]{1,0:T(8,128)(2,1)} fusion(bf16[1,720,2304]{2,1,0:T(8,128)(2,1)S(1)} %copy-done, f32[640,720]{0,1:T(8,128)} %fusion.3, bf16[1,2304,720]{1,2,0:T(8,128)(2,1)} %param.28, bf16[640,1152]{1,0:T(8,128)(2,1)} %bitcast.99, bf16[640,1152]{1,0:T(8,128)(2,1)} %bitcast.85, pred[]{:T(512)S(6)} %eq.118), kind=kOutput, calls=%fused_computation.3 | convolution fusion | flops 4264243200 | bytes 14376961 | tf_op jit(solution)/shard_map/dot_general | solution.py:147
  284.1 5.5 %copy.48 = bf16[640,2304]{0,1:T(8,128)(2,1)} copy(bf16[640,2304]{1,0:T(8,128)(2,1)} %convolution_convert_fusion) | data formatting | bytes 5898240 | tf_op jit(solution)/shard_map/convert_element_type | solution.py:149
  291.7 2.9 collective-permute-done.3
  296.1 4.6 %copy.49 = bf16[640,4,288]{2,1,0:T(4,128)(2,1)} copy(bf16[640,4,288]{0,2,1:T(8,128)(2,1)} %fusion.5) | data formatting | bytes 2949120 | tf_op jit(solution)/shard_map/convert_element_type | solution.py:155
  300.7 4.2 %reshape.298 = bf16[8,80,1152]{2,1,0:T(8,128)(2,1)} reshape(bf16[640,4,288]{2,1,0:T(4,128)(2,1)} %copy.49) | data formatting | bytes 2949120 | tf_op jit(solution)/shard_map/reshape | solution.py:157
  304.9 9.8 %all-to-all-start.1 = ((bf16[8,80,1152]{2,1,0:T(8,128)(2,1)}), bf16[8,80,1152]{2,1,0:T(8,128)(2,1)}, u32[]{:S(2)}, u32[]{:S(2)}) async-start(bf16[8,80,1152]{2,1,0:T(8,128)(2,1)} %reshape.298), calls=%async_computation.1 | async-start | bytes 2949120 | tf_op jit(solution)/shard_map/all_to_all | solution.py:156
  317.2 21.4 %all-to-all-done.1 = bf16[8,80,1152]{2,1,0:T(8,128)(2,1)} async-done(((bf16[8,80,1152]{2,1,0:T(8,128)(2,1)}), bf16[8,80,1152]{2,1,0:T(8,128)(2,1)}, u32[]{:S(2)}, u32[]{:S(2)}) %all-to-all-start.1) | async-done | bytes 1474592 | tf_op jit(solution)/shard_map/all_to_all | solution.py:156
  338.6 4.1 %fusion.6 = bf16[256,1152]{0,1:T(8,128)(2,1)} fusion(bf16[8,80,1152]{2,1,0:T(8,128)(2,1)} %all-to-all-done.1, f32[8,256]{1,0:T(8,128)S(1)} %select_add_fusion, s32[8,256]{1,0:T(8,128)S(1)} %add_bitcast_fusion, pred[8,256]{1,0:T(8,128)(4,1)S(1)} %fusion.26), kind=kOutput, calls=%fused_computation.14 | convolution fusion | flops 2265710592 | bytes 2082816 | tf_op jit(solution)/shard_map/est,esd->td/dot_general | solution.py:167
  342.7 38.4 %reduce-scatter.2.cloned.1.call-done = bf16[256,288]{0,1:T(8,128)(2,1)} async-done(((bf16[256,1152]{0,1:T(8,128)(2,1)}), bf16[256,288]{0,1:T(8,128)(2,1)}) %reduce-scatter.2.cloned.1.call-update) | async-done | bytes 147472 | tf_op jit(solution)/shard_map/reduce_scatter | solution.py:174
  (80 shorter events, 45.3 us)
Async XLA Ops:
  6.5 262.1 %copy-start = (bf16[1,720,2304]{2,1,0:T(8,128)(2,1)S(1)}, bf16[1,720,2304]{2,1,0:T(8,128)(2,1)}, u32[]{:S(2)}) copy-start(bf16[1,720,2304]{2,1,0:T(8,128)(2,1)} %param.29) | copy-start | bytes 9953284
  6.5 86.7 %all-gather.3.cloned.1.call-start = ((), (), s32[]{:S(2)}) async-start(), calls=%async_computation.5 | async-start | bytes 1216512 | tf_op jit(solution)/shard_map/all_gather | solution.py:89
  9.4 187.2 %all-reduce.2.cloned.1.call-start = ((), (), s32[]{:S(2)}) async-start(), calls=%async_computation.3 | async-start | bytes 1179648 | tf_op jit(solution)/shard_map/psum | solution.py:45
  17.2 86.1 %copy-start.5 = (bf16[256,288]{0,1:T(8,128)(2,1)S(1)}, bf16[256,288]{0,1:T(8,128)(2,1)}, u32[]{:S(2)}) copy-start(bf16[256,288]{0,1:T(8,128)(2,1)} %param.16) | copy-start | bytes 442372
  142.3 9.9 %copy-start.8 = (s32[256,2]{0,1:T(2,128)S(1)}, s32[256,2]{0,1:T(2,128)}, u32[]{:S(2)}) copy-start(s32[256,2]{0,1:T(2,128)} %param.26) | copy-start | bytes 6148
  142.3 57.6 %copy-start.7 = (bf16[2304]{0:T(1024)(128)(2,1)S(1)}, bf16[2304]{0:T(1024)(128)(2,1)}, u32[]{:S(2)}) copy-start(bf16[2304]{0:T(1024)(128)(2,1)} %param.24) | copy-start | bytes 13828
  144.3 5.7 %collective-permute-start = (bf16[256,4,288]{0,2,1:T(8,128)(2,1)}, bf16[256,4,288]{0,2,1:T(8,128)(2,1)}, u32[]{:S(2)}, u32[]{:S(2)}) collective-permute-start(bf16[256,4,288]{0,2,1:T(8,128)(2,1)} %dynamic-slice_bitcast_fusion.1), channel_id=1, source_target_pairs={{0,1},{1,0},{2,3},{3,2},{4,5},{5,4},{6,7},{7,6},{8,9},{9,8},{10,11... | collective-permute-start | bytes 1769480 | tf_op jit(solution)/shard_map/ppermute | solution.py:43
  196.5 6.0 %collective-permute-start.1 = (bf16[256,4,288]{0,2,1:T(8,128)(2,1)}, bf16[256,4,288]{0,2,1:T(8,128)(2,1)}, u32[]{:S(2)}, u32[]{:S(2)}) collective-permute-start(bf16[256,4,288]{0,2,1:T(8,128)(2,1)} %all-reduce.2.cloned.1.call-done), channel_id=1, source_target_pairs={{0,1},{1,0},{2,3},{3,2},{4,5},{5,4},{6,7},{7,6},{8,9},{9,8},{10,11... | collective-permute-start | bytes 1769480 | tf_op jit(solution)/shard_map/ppermute | solution.py:46
  204.5 1.3 copy-start.3
  206.2 1.4 copy-start.1
  221.8 42.7 %copy-start.9 = (bf16[1,2304,720]{1,2,0:T(8,128)(2,1)S(1)}, bf16[1,2304,720]{1,2,0:T(8,128)(2,1)}, u32[]{:S(2)}) copy-start(bf16[1,2304,720]{1,2,0:T(8,128)(2,1)} %param.27) | copy-start | bytes 9953284
  259.1 4.3 %copy-start.4 = (bf16[8,80,1152]{2,1,0:T(8,128)(2,1)}, bf16[8,80,1152]{2,1,0:T(8,128)(2,1)S(1)}, u32[]{:S(2)}) copy-start(bf16[8,80,1152]{2,1,0:T(8,128)(2,1)S(1)} %all_to_all.10) | copy-start | bytes 4423684
  259.1 4.3 %collective-permute-start.2 = (bf16[8,80,1152]{2,1,0:T(8,128)(2,1)S(1)}, bf16[8,80,1152]{2,1,0:T(8,128)(2,1)S(1)}, u32[]{:S(2)}, u32[]{:S(2)}) collective-permute-start(bf16[8,80,1152]{2,1,0:T(8,128)(2,1)S(1)} %all_to_all.10), channel_id=1, source_target_pairs={{0,1},{1,0},{2,3},{3,2},{4,5},{5,4},{6,7},{7,6},{8,9},{9,8},{10,11... | collective-permute-start | bytes 4423688 | tf_op jit(solution)/shard_map/ppermute | solution.py:137
  263.4 1.2 copy-start.10
  289.6 5.0 %copy-start.2 = (bf16[640,2304]{0,1:T(8,128)(2,1)S(1)}, bf16[640,2304]{0,1:T(8,128)(2,1)}, u32[]{:S(2)}) copy-start(bf16[640,2304]{0,1:T(8,128)(2,1)} %copy.48) | copy-start | bytes 8847364
  291.2 3.4 collective-permute-start.3
  300.7 14.3 %copy-start.6 = (bf16[2304,8]{0,1:T(8,128)(2,1)S(1)}, bf16[2304,8]{0,1:T(8,128)(2,1)}, u32[]{:S(2)}) copy-start(bf16[2304,8]{0,1:T(8,128)(2,1)} %param.25) | copy-start | bytes 110596
  304.9 33.7 %all-to-all-start.1 = ((bf16[8,80,1152]{2,1,0:T(8,128)(2,1)}), bf16[8,80,1152]{2,1,0:T(8,128)(2,1)}, u32[]{:S(2)}, u32[]{:S(2)}) async-start(bf16[8,80,1152]{2,1,0:T(8,128)(2,1)} %reshape.298), calls=%async_computation.1 | async-start | bytes 2949120 | tf_op jit(solution)/shard_map/all_to_all | solution.py:156
  314.7 66.4 %reduce-scatter.2.cloned.1.call-start = ((), (), s32[]{:S(2)}) async-start(), calls=%async_computation.4 | async-start | bytes 737280 | tf_op jit(solution)/shard_map/reduce_scatter | solution.py:174
Sparse Core Ops, SparseCore 0:
  10.8 82.3 all-gather.2
  152.4 44.0 all-reduce.1
  342.8 38.2 reduce-scatter.1
